TPU v7x, 128 devices: a whole 4x4x4 slice. The times are simulated.
128 devices in a mesh: tp: 4 (over y_lo, core), dp: 32 (over x, z, y_hi).
Axes of the slice: x: 4, y: 4 (y_hi: 2, y_lo: 2; y = y_hi * 2 + y_lo), z: 4, core: 2. Of those that a mesh axis runs over, the one named last changes fastest.
Arguments:
- teacher_query: bfloat16 [8192, 8192], P('dp', 'tp'), may hold values from -8 to 8
- student_hidden: bfloat16 [8192, 4096], P('dp', 'tp'), may hold values from -16 to 16
- query_weight: bfloat16 [4096, 4096], P('dp', 'tp'), may hold values from -0.039794922 to 0.039794922
Outputs:
- kl_rows: float32 [128, 2048], P(('tp', 'dp'))
- weight_grad: float32 [4096, 4096], P('dp', 'tp')
All inputs are finite; a program needn't handle non-finite values.
Results may differ from a plain program's by a relative error of at most 0.0029.
Values may be sent and summed in bfloat16 or wider, within the bound.
No kernel may reach another device: no remote copies, remote signals or barrier semaphores. Data moves between devices by JAX's collectives and lax.ppermute only.
A program may use at most 64 MiB of HBM per device.

v0:
```python
import jax
import jax.numpy as jnp
from jax import lax
from jax.sharding import PartitionSpec as P

RHEADS = 32
NSEQ = 2
SEQ = 4096


def from_everyone(value, axis):
    copies = jnp.broadcast_to(value, (lax.axis_size(axis), *value.shape))
    return lax.all_to_all(copies, axis, split_axis=0, concat_axis=0, tiled=True)


def laid_out(parts, dim):
    lengths = list(parts.shape[1:])
    lengths[dim] *= parts.shape[0]
    return jnp.moveaxis(parts, 0, dim).reshape(lengths)


def gather_directly(value, axis, dim):
    parts = from_everyone(value, axis)
    return laid_out(parts, dim)


def in_one_piece(arrays, axis, split_dim, concat_dim, along):
    ends, at = ([], 0)
    for a in arrays[:-1]:
        at += a.shape[along]
        ends.append(at)
    both = jnp.concatenate(arrays, axis=along)
    return tuple(
        jnp.split(
            lax.all_to_all(both, axis, split_axis=split_dim, concat_axis=concat_dim, tiled=True),
            ends,
            axis=along,
        )
    )


def spread_heads(queries, heads, copies):
    rows = queries.shape[0]
    width = queries.shape[1] // heads
    shaped = queries.reshape(rows, heads, 1, width)
    return jnp.broadcast_to(shaped, (rows, heads, copies, width)).reshape(
        rows, heads * copies, width
    )


def local(teacher_query, student_hidden, query_weight):
    heads_here = RHEADS // lax.axis_size("tp")
    copies = lax.axis_size("dp") // heads_here
    rows = teacher_query.shape[0]
    teacher_width = teacher_query.shape[1] // heads_here
    hidden_full = gather_directly(student_hidden, "tp", 1)
    teacher_send = spread_heads(teacher_query, heads_here, copies)
    projected = jnp.dot(
        hidden_full,
        lax.all_gather(query_weight, "dp", axis=0, tiled=True),
        preferred_element_type=jnp.float32,
    )
    student_query = projected.astype(jnp.bfloat16)
    student_width = student_query.shape[1] // heads_here
    student_send = spread_heads(student_query, heads_here, copies)
    teacher_all, student_all = in_one_piece((teacher_send, student_send), "dp", 1, 0, 2)
    total_rows = teacher_all.shape[0]
    teacher_all = teacher_all.reshape(total_rows, teacher_width)
    student_all = student_all.reshape(total_rows, student_width)
    teacher_scale = teacher_width ** (-0.5)
    student_scale = student_width ** (-0.5)
    query_rows = SEQ // copies
    first_row = lax.axis_index("dp") % copies * query_rows
    block = min(512, query_rows)
    blocks_each = query_rows // block

    def relation_step(step, carry):
        kl_store, grad_store = carry
        sequence = step // blocks_each
        offset = step % blocks_each * block
        base = sequence * SEQ
        start = base + first_row + offset
        teacher_keys = lax.dynamic_slice_in_dim(teacher_all, base, SEQ, 0)
        student_keys = lax.dynamic_slice_in_dim(student_all, base, SEQ, 0)
        teacher_rows = lax.dynamic_slice_in_dim(teacher_all, start, block, 0)
        student_rows = lax.dynamic_slice_in_dim(student_all, start, block, 0)
        teacher_scores = (
            lax.dot_general(
                teacher_rows,
                teacher_keys,
                (((1,), (1,)), ((), ())),
                preferred_element_type=jnp.float32,
            )
            * teacher_scale
        )
        student_scores = (
            lax.dot_general(
                student_rows,
                student_keys,
                (((1,), (1,)), ((), ())),
                preferred_element_type=jnp.float32,
            )
            * student_scale
        )
        teacher_log = jax.nn.log_softmax(teacher_scores, axis=-1)
        student_log = jax.nn.log_softmax(student_scores, axis=-1)
        teacher_prob = jnp.exp(teacher_log)
        divergence = jnp.sum(teacher_prob * (teacher_log - student_log), axis=-1)
        score_grad = (jnp.exp(student_log) - teacher_prob).astype(jnp.bfloat16)
        key_part = (
            lax.dot_general(
                score_grad,
                student_rows,
                (((0,), (0,)), ((), ())),
                preferred_element_type=jnp.float32,
            )
            * student_scale
        )
        row_part = (
            jnp.dot(score_grad, student_keys, preferred_element_type=jnp.float32) * student_scale
        )
        seq_grad = lax.dynamic_slice_in_dim(grad_store, base, SEQ, 0)
        grad_store = lax.dynamic_update_slice_in_dim(grad_store, seq_grad + key_part, base, 0)
        current = lax.dynamic_slice_in_dim(grad_store, start, block, 0)
        grad_store = lax.dynamic_update_slice_in_dim(grad_store, current + row_part, start, 0)
        kl_store = lax.dynamic_update_slice_in_dim(
            kl_store, divergence, sequence * query_rows + offset, 0
        )
        return (kl_store, grad_store)

    kl_init = jnp.zeros((NSEQ * query_rows,), jnp.float32)
    grad_init = jnp.zeros((total_rows, student_width), jnp.float32)
    kl_store, grad_store = lax.fori_loop(0, NSEQ * blocks_each, relation_step, (kl_init, grad_init))
    returned = lax.all_to_all(
        grad_store.reshape(heads_here * copies, rows, student_width),
        "dp",
        split_axis=0,
        concat_axis=2,
        tiled=True,
    )
    summed = jnp.sum(returned.reshape(rows, heads_here, copies, student_width), axis=2)
    query_grad = summed.reshape(rows, heads_here * student_width).astype(jnp.bfloat16)
    feature_block = lax.all_to_all(hidden_full, "dp", split_axis=1, concat_axis=0, tiled=True)
    weight_grad = lax.dot_general(
        feature_block,
        lax.all_gather(query_grad, "dp", axis=0, tiled=True),
        (((0,), (0,)), ((), ())),
        preferred_element_type=jnp.float32,
    )
    return (kl_store.reshape(1, NSEQ * query_rows), weight_grad)


def solution(mesh):
    placed = (P("dp", "tp"), P("dp", "tp"), P("dp", "tp"))
    return jax.shard_map(
        local,
        mesh=mesh,
        in_specs=placed,
        out_specs=(P(("tp", "dp"), None), P("dp", "tp")),
        check_vma=False,
    )
```

profile of v0, /device:TPU:1, one launch (start us, length us, event | category | flops | bytes accessed | tf_op | source)
XLA Modules:
  0.0 572.4 jit_solution(10103598577909109360)
XLA Ops:
  10.7 5.0 all-to-all-start
  17.0 25.4 %all-to-all-done = bf16[4,256,1024]{1,2,0:T(8,128)(2,1)S(1)} async-done(((bf16[4,256,1024]{1,2,0:T(8,128)(2,1)}), bf16[4,256,1024]{1,2,0:T(8,128)(2,1)S(1)}, u32[]{:S(2)}, u32[]{:S(2)}) %all-to-all-start) | async-done | bytes 2097184 | tf_op jit(solution)/shard_map/all_to_all | solution.py:13
  42.4 77.6 %all-gather.3.cloned.1.call-done = bf16[4096,1024]{1,0:T(8,128)(2,1)} async-done(((bf16[128,1024]{1,0:T(8,128)(2,1)}), bf16[4096,1024]{1,0:T(8,128)(2,1)}) %all-gather.3.cloned.1.call-update) | async-done | bytes 8388624 | tf_op jit(solution)/shard_map/all_gather | solution.py:60
  120.0 5.7 %fusion.16 = bf16[32,8,8,128]{3,2,1,0:T(8,128)(2,1)S(1)} fusion(bf16[256,4096]{0,1:T(8,128)(2,1)S(1)} %bitcast.49, bf16[4096,1024]{1,0:T(8,128)(2,1)} %all-gather.3.cloned.1.call-done), kind=kOutput, calls=%fused_computation.32 | convolution fusion | flops 2147745792 | bytes 11010048 | tf_op jit(solution)/shard_map/dot_general | solution.py:58
  126.9 3.4 pad_maximum_fusion
  130.3 5.4 all-to-all-start.1
  135.9 97.5 %all-to-all-done.1 = bf16[256,32,384]{2,0,1:T(8,128)(2,1)} async-done(((bf16[256,32,384]{2,0,1:T(8,128)(2,1)}), bf16[256,32,384]{2,0,1:T(8,128)(2,1)}, u32[]{:S(2)}, u32[]{:S(2)}) %all-to-all-start.1) | async-done | bytes 6291488 | tf_op jit(solution)/shard_map/all_to_all | solution.py:35
  235.1 4.5 slice_bitcast_fusion
  242.0 87.4 %while.17 = (s32[]{:T(128)}, f32[2048]{0:T(1024)S(1)}, f32[8192,128]{1,0:T(8,128)}, s32[]{:T(128)}, bf16[8192,256]{1,0:T(8,128)(2,1)}, /*index=5*/bf16[8192,128]...) while((s32[]{:T(128)}, f32[2048]{0:T(1024)S(1)}, ...), condition=%wide.region_4.6_spmd, body=%wide.region_0.5_spmd.sunk | while | flops 2729571840 | bytes 89164272 | solution.py:133
  242.0 3.1 multiply_reduce_fusion.5
  249.4 5.7 subtract_convert_fusion.2
  255.3 5.6 fusion.33
  271.2 5.7 subtract_convert_fusion.2
  277.1 5.6 fusion.33
  293.1 5.7 subtract_convert_fusion.2
  298.9 5.6 fusion.33
  307.5 3.1 multiply_reduce_fusion.5
  314.9 5.7 subtract_convert_fusion.2
  320.8 5.6 fusion.33
  329.3 54.7 %all_to_all.57 = f32[32,256,128]{2,1,0:T(8,128)S(1)} all-to-all(f32[32,256,128]{2,1,0:T(8,128)} %bitcast.48), channel_id=1, replica_groups=mesh['tp'=4,'dp'=32] {'dp'}, dimensions={0} | all-to-all | bytes 8388608 | tf_op jit(solution)/shard_map/all_to_all | solution.py:134
  385.4 37.5 %all_to_all.58 = bf16[256,32,128]{0,2,1:T(8,128)(2,1)} all-to-all(bf16[256,32,128]{0,2,1:T(8,128)(2,1)S(1)} %bitcast.50), channel_id=1, replica_groups=mesh['tp'=4,'dp'=32] {'dp'}, dimensions={1} | all-to-all | bytes 4194304 | tf_op jit(solution)/shard_map/all_to_all | solution.py:143
  422.8 3.2 copy.22
  426.1 130.4 %all-gather.5.cloned.1.call-done = bf16[8192,1024]{0,1:T(8,128)(2,1)} async-done(((bf16[256,1024]{0,1:T(8,128)(2,1)}), bf16[8192,1024]{0,1:T(8,128)(2,1)}) %all-gather.5.cloned.1.call-update) | async-done | bytes 16777232 | tf_op jit(solution)/shard_map/all_gather | solution.py:146
  556.5 8.1 %convolution_bitcast_fusion = f32[128,1024]{0,1:T(8,128)S(1)} fusion(bf16[8192,1024]{0,1:T(8,128)(2,1)} %all-gather.5.cloned.1.call-done, bf16[8192,128]{1,0:T(8,128)(2,1)S(1)} %bitcast.56), kind=kOutput, calls=%fused_computation.33 | convolution fusion | flops 2147483648 | bytes 19398656 | tf_op jit(solution)/shard_map/dot_general | solution.py:144
  (60 shorter events, 48.5 us)
Async XLA Ops:
  7.2 112.8 %all-gather.3.cloned.1.call-start = ((), (), s32[]{:S(2)}) async-start(), calls=%async_computation.4 | async-start | bytes 8650752 | tf_op jit(solution)/shard_map/all_gather | solution.py:60
  10.7 31.7 %all-to-all-start = ((bf16[4,256,1024]{1,2,0:T(8,128)(2,1)}), bf16[4,256,1024]{1,2,0:T(8,128)(2,1)S(1)}, u32[]{:S(2)}, u32[]{:S(2)}) async-start(bf16[4,256,1024]{1,2,0:T(8,128)(2,1)} %broadcast_in_dim.29), calls=%async_computation | async-start | bytes 4194304 | tf_op jit(solution)/shard_map/all_to_all | solution.py:13
  42.4 83.4 %copy-start.1 = (bf16[4,256,1024]{1,2,0:T(8,128)(2,1)}, bf16[4,256,1024]{1,2,0:T(8,128)(2,1)S(1)}, u32[]{:S(2)}) copy-start(bf16[4,256,1024]{1,2,0:T(8,128)(2,1)S(1)} %all-to-all-done) | copy-start | bytes 6291460
  130.3 103.1 %all-to-all-start.1 = ((bf16[256,32,384]{2,0,1:T(8,128)(2,1)}), bf16[256,32,384]{2,0,1:T(8,128)(2,1)}, u32[]{:S(2)}, u32[]{:S(2)}) async-start(bf16[256,32,384]{2,0,1:T(8,128)(2,1)} %pad_maximum_fusion), calls=%async_computation.1 | async-start | bytes 12582912 | tf_op jit(solution)/shard_map/all_to_all | solution.py:35
  135.7 420.8 %all-gather.5.cloned.1.call-start = ((), (), s32[]{:S(2)}) async-start(), calls=%async_computation.5 | async-start | bytes 17301504 | tf_op jit(solution)/shard_map/all_gather | solution.py:146
  255.3 5.6 copy-start
  277.1 5.6 copy-start
  298.9 5.6 copy-start
  320.8 5.6 copy-start
  329.3 55.0 %copy-start.3 = (f32[2048]{0:T(1024)}, f32[2048]{0:T(1024)S(1)}, u32[]{:S(2)}) copy-start(f32[2048]{0:T(1024)S(1)} %get-tuple-element.161) | copy-start | bytes 24580
  329.3 56.0 %copy-start.2 = (bf16[4,256,1024]{1,2,0:T(8,128)(2,1)S(1)}, bf16[4,256,1024]{1,2,0:T(8,128)(2,1)}, u32[]{:S(2)}) copy-start(bf16[4,256,1024]{1,2,0:T(8,128)(2,1)} %copy-done.1) | copy-start | bytes 6291460
Sparse Core Ops, SparseCore 0:
  11.0 108.9 all-gather.2
  385.5 170.9 all-gather.4
where the time goes:
time: 573 us; the launch traced here: 572 us
  waiting for transfers between devices  332 us (58%)
  blocking collectives  92.2 us (16%)
  matrix products  65.7 us (11%)
  other arithmetic  38.4 us (7%)
  local copies, waits for them, and re-layouts  19.7 us (3%)
  between operations  14.2 us (2%)
  starting transfers between devices  10.6 us (2%)
    all_gather x1, waiting for transfers between devices, local(): lax.all_gather(query_grad, 'dp', axis=0, tiled=True)  130 us
    all_to_all x1, waiting for transfers between devices, in_one_piece(): lax.all_to_all(both, axis, split_axis=split_dim, concat_axis=concat_dim,...  97.5 us
    all_gather x1, waiting for transfers between devices, local(): lax.all_gather(query_weight, 'dp', axis=0, tiled=True)  77.6 us
    all_to_all x1, blocking collectives, local(): lax.all_to_all(grad_store.reshape(heads_here * copies, rows, student_widt...  54.7 us
    all_to_all x1, blocking collectives, local(): lax.all_to_all(hidden_full, 'dp', split_axis=1, concat_axis=0, tiled=True)  37.5 us
    all_to_all x1, waiting for transfers between devices, from_everyone(): return lax.all_to_all(copies, axis, split_axis=0, concat_axis=0, tiled=True)  25.4 us
    convert_element_type x4, other arithmetic, relation_step(): score_grad = (jnp.exp(student_log) - teacher_prob).astype(jnp.bfloat16)  22.7 us
    dot_general x4, matrix products, relation_step(): lax.dot_general(score_grad, student_rows, (((0,), (0,)), ((), ())), prefe...  22.5 us
  transfers between devices with their start and end apart: 4, of which 4 were waited for; matrix products, arithmetic and copies ran while one was open for 1% of the time, Pallas kernels for 0%

commit v1 on v0

--- a/solution.py
+++ b/solution.py
@@ -49,6 +49,17 @@
 
 
 def local(teacher_query, student_hidden, query_weight):
+
+    def reach_target(row_data):
+        carry_out = lax.all_to_all(
+            jnp.stack([row_data] * lax.axis_size("dp"), axis=0),
+            axis_name="dp",
+            concat_axis=0,
+            split_axis=0,
+        )
+        val = jnp.concatenate(carry_out, 0)
+        return val
+
     heads_here = RHEADS // lax.axis_size("tp")
     copies = lax.axis_size("dp") // heads_here
     rows = teacher_query.shape[0]
@@ -143,7 +154,7 @@
     feature_block = lax.all_to_all(hidden_full, "dp", split_axis=1, concat_axis=0, tiled=True)
     weight_grad = lax.dot_general(
         feature_block,
-        lax.all_gather(query_grad, "dp", axis=0, tiled=True),
+        reach_target(query_grad),
         (((0,), (0,)), ((), ())),
         preferred_element_type=jnp.float32,
     )

time: 573 us -> 646 us (1.13); the launches traced: 572 us -> 634 us
  blocking collectives: 92.2 us -> 193 us
  waiting for transfers between devices: 332 us -> 278 us
  starting transfers between devices: 10.6 us -> 25.8 us
    all_gather x1 -> x0, waiting for transfers between devices: 130 us -> none  [local(): lax.all_gather(query_grad, 'dp', axis=0, tiled=True)]
    all_to_all x2 -> x1, blocking collectives: 92.2 us -> 193 us  [reach_target(): lax.all_to_all(jnp.stack([row_data] * lax.axis_size('dp'), axis=0), axis_...]
    all_to_all x0 -> x2, waiting for transfers between devices: none -> 75.6 us  [the longest x1 48.9 us: local(): lax.all_to_all(grad_store.reshape(heads_here * copies, rows, student_widt...]
    all_to_all x0 -> x2, starting transfers between devices: none -> 15.2 us  [the longest x1 10 us: local(): lax.all_to_all(hidden_full, 'dp', split_axis=1, concat_axis=0, tiled=True)]
  transfers between devices with their start and end apart: 4 -> 5, of which waited for: 4 -> 5; matrix products, arithmetic and copies ran while one was open for 1% -> 2% of each run, Pallas kernels for 0% -> 0%
where the time goes in v1:
time: 646 us; the launch traced here: 634 us
  waiting for transfers between devices  278 us (43%)
  blocking collectives  193 us (30%)
  matrix products  62 us (10%)
  other arithmetic  40.8 us (6%)
  starting transfers between devices  25.8 us (4%)
  local copies, waits for them, and re-layouts  20.5 us (3%)
  between operations  14.2 us (2%)
    all_to_all x1, blocking collectives, reach_target(): lax.all_to_all(jnp.stack([row_data] * lax.axis_size('dp'), axis=0), axis_...  193 us
    all_to_all x1, waiting for transfers between devices, in_one_piece(): lax.all_to_all(both, axis, split_axis=split_dim, concat_axis=concat_dim,...  98.4 us
    all_gather x1, waiting for transfers between devices, local(): lax.all_gather(query_weight, 'dp', axis=0, tiled=True)  77.7 us
    all_to_all x1, waiting for transfers between devices, local(): lax.all_to_all(grad_store.reshape(heads_here * copies, rows, student_widt...  48.9 us
    all_to_all x1, waiting for transfers between devices, local(): lax.all_to_all(hidden_full, 'dp', split_axis=1, concat_axis=0, tiled=True)  26.7 us
    all_to_all x1, waiting for transfers between devices, from_everyone(): return lax.all_to_all(copies, axis, split_axis=0, concat_axis=0, tiled=True)  25.4 us
    convert_element_type x4, other arithmetic, relation_step(): score_grad = (jnp.exp(student_log) - teacher_prob).astype(jnp.bfloat16)  22.6 us
    dot_general x4, matrix products, relation_step(): lax.dot_general(score_grad, student_rows, (((0,), (0,)), ((), ())), prefe...  22.4 us
  transfers between devices with their start and end apart: 5, of which 5 were waited for; matrix products, arithmetic and copies ran while one was open for 2% of the time, Pallas kernels for 0%

profile of v1, /device:TPU:1, one launch (start us, length us, event | category | flops | bytes accessed | tf_op | source)
XLA Modules:
  0.0 634.0 jit_solution(11472864168270042675)
XLA Ops:
  10.7 5.0 all-to-all-start
  16.9 25.4 %all-to-all-done = bf16[4,256,1024]{1,2,0:T(8,128)(2,1)S(1)} async-done(((bf16[4,256,1024]{1,2,0:T(8,128)(2,1)}), bf16[4,256,1024]{1,2,0:T(8,128)(2,1)S(1)}, u32[]{:S(2)}, u32[]{:S(2)}) %all-to-all-start) | async-done | bytes 2097184 | tf_op jit(solution)/shard_map/all_to_all | solution.py:13
  42.4 77.7 %all-gather.2.cloned.1.call-done = bf16[4096,1024]{1,0:T(8,128)(2,1)} async-done(((bf16[128,1024]{1,0:T(8,128)(2,1)}), bf16[4096,1024]{1,0:T(8,128)(2,1)}) %all-gather.2.cloned.1.call-update) | async-done | bytes 8388624 | tf_op jit(solution)/shard_map/all_gather | solution.py:71
  120.0 5.7 fusion.18
  126.9 3.4 pad_maximum_fusion
  130.3 5.6 all-to-all-start.1
  135.9 98.4 %all-to-all-done.1 = bf16[256,32,384]{2,0,1:T(8,128)(2,1)} async-done(((bf16[256,32,384]{2,0,1:T(8,128)(2,1)}), bf16[256,32,384]{2,0,1:T(8,128)(2,1)}, u32[]{:S(2)}, u32[]{:S(2)}) %all-to-all-start.1) | async-done | bytes 6291488 | tf_op jit(solution)/shard_map/all_to_all | solution.py:35
  236.0 4.5 slice_bitcast_fusion
  242.8 87.3 %while.17 = (s32[]{:T(128)}, f32[2048]{0:T(1024)S(1)}, f32[8192,128]{1,0:T(8,128)}, s32[]{:T(128)}, bf16[8192,256]{1,0:T(8,128)(2,1)}, /*index=5*/bf16[8192,128]...) while((s32[]{:T(128)}, f32[2048]{0:T(1024)S(1)}, ...), condition=%wide.region_4.6_spmd, body=%wide.region_0.5_spmd.sunk | while | flops 2729571840 | bytes 89164272 | solution.py:144
  250.3 5.7 subtract_convert_fusion.2
  256.1 5.6 fusion.37
  272.1 5.7 subtract_convert_fusion.2
  277.9 5.6 fusion.37
  286.5 3.1 multiply_reduce_fusion.5
  293.9 5.7 subtract_convert_fusion.2
  299.7 5.6 fusion.37
  315.7 5.7 subtract_convert_fusion.2
  321.6 5.6 fusion.37
  330.1 5.2 all-to-all-start.2
  338.2 48.9 %all-to-all-done.2 = f32[32,256,128]{2,1,0:T(8,128)} async-done(((f32[32,256,128]{2,1,0:T(8,128)}), f32[32,256,128]{2,1,0:T(8,128)}, u32[]{:S(2)}, u32[]{:S(2)}) %all-to-all-start.2) | async-done | bytes 4194336 | tf_op jit(solution)/shard_map/all_to_all | solution.py:145
  387.1 10.0 %all-to-all-start.4 = ((bf16[256,32,128]{2,0,1:T(8,128)(2,1)}), bf16[256,32,128]{2,0,1:T(8,128)(2,1)S(1)}, u32[]{:S(2)}, u32[]{:S(2)}) async-start(bf16[256,32,128]{2,0,1:T(8,128)(2,1)} %copy.22), calls=%async_computation.4 | async-start | bytes 4194304 | tf_op jit(solution)/shard_map/all_to_all | solution.py:154
  400.0 26.7 %all-to-all-done.4 = bf16[256,32,128]{2,0,1:T(8,128)(2,1)S(1)} async-done(((bf16[256,32,128]{2,0,1:T(8,128)(2,1)}), bf16[256,32,128]{2,0,1:T(8,128)(2,1)S(1)}, u32[]{:S(2)}, u32[]{:S(2)}) %all-to-all-start.4) | async-done | bytes 2097184 | tf_op jit(solution)/shard_map/all_to_all | solution.py:154
  428.7 193.0 %all_to_all.59 = bf16[32,256,1024]{1,2,0:T(8,128)(2,1)S(1)} all-to-all(bf16[32,256,1024]{1,2,0:T(8,128)(2,1)S(1)} %stack.2), channel_id=1, replica_groups=mesh['tp'=4,'dp'=32] {'dp'}, dimensions={0} | all-to-all | bytes 33554432 | tf_op jit(solution)/shard_map/all_to_all | solution.py:54
  621.7 4.5 fusion.19
  (61 shorter events, 57.7 us)
Async XLA Ops:
  7.2 112.9 %all-gather.2.cloned.1.call-start = ((), (), s32[]{:S(2)}) async-start(), calls=%async_computation.5 | async-start | bytes 8650752 | tf_op jit(solution)/shard_map/all_gather | solution.py:71
  10.7 31.7 %all-to-all-start = ((bf16[4,256,1024]{1,2,0:T(8,128)(2,1)}), bf16[4,256,1024]{1,2,0:T(8,128)(2,1)S(1)}, u32[]{:S(2)}, u32[]{:S(2)}) async-start(bf16[4,256,1024]{1,2,0:T(8,128)(2,1)} %broadcast_in_dim.29), calls=%async_computation | async-start | bytes 4194304 | tf_op jit(solution)/shard_map/all_to_all | solution.py:13
  42.4 83.4 %copy-start.1 = (bf16[4,256,1024]{1,2,0:T(8,128)(2,1)}, bf16[4,256,1024]{1,2,0:T(8,128)(2,1)S(1)}, u32[]{:S(2)}) copy-start(bf16[4,256,1024]{1,2,0:T(8,128)(2,1)S(1)} %all-to-all-done) | copy-start | bytes 6291460
  130.3 104.0 %all-to-all-start.1 = ((bf16[256,32,384]{2,0,1:T(8,128)(2,1)}), bf16[256,32,384]{2,0,1:T(8,128)(2,1)}, u32[]{:S(2)}, u32[]{:S(2)}) async-start(bf16[256,32,384]{2,0,1:T(8,128)(2,1)} %pad_maximum_fusion), calls=%async_computation.1 | async-start | bytes 12582912 | tf_op jit(solution)/shard_map/all_to_all | solution.py:35
  256.1 5.6 copy-start
  277.9 5.6 copy-start
  299.7 5.6 copy-start
  321.6 5.6 copy-start
  330.1 8.1 %copy-start.3 = (f32[2048]{0:T(1024)}, f32[2048]{0:T(1024)S(1)}, u32[]{:S(2)}) copy-start(f32[2048]{0:T(1024)S(1)} %get-tuple-element.161) | copy-start | bytes 24580
  330.1 5.2 copy-start.2
  330.1 57.0 %all-to-all-start.2 = ((f32[32,256,128]{2,1,0:T(8,128)}), f32[32,256,128]{2,1,0:T(8,128)}, u32[]{:S(2)}, u32[]{:S(2)}) async-start(f32[32,256,128]{2,1,0:T(8,128)} %bitcast.52), calls=%async_computation.2 | async-start | bytes 8388608 | tf_op jit(solution)/shard_map/all_to_all | solution.py:145
  387.1 39.6 %all-to-all-start.4 = ((bf16[256,32,128]{2,0,1:T(8,128)(2,1)}), bf16[256,32,128]{2,0,1:T(8,128)(2,1)S(1)}, u32[]{:S(2)}, u32[]{:S(2)}) async-start(bf16[256,32,128]{2,0,1:T(8,128)(2,1)} %copy.22), calls=%async_computation.4 | async-start | bytes 4194304 | tf_op jit(solution)/shard_map/all_to_all | solution.py:154
Sparse Core Ops, SparseCore 0:
  11.0 108.9 all-gather.1
